TPU v7x, 256 devices: a whole 4x4x8 slice. The times are simulated.
256 devices in a mesh: dp: 32 (over z, x_hi, core), seq: 8 (over y, x_lo).
Axes of the slice: x: 4 (x_hi: 2, x_lo: 2; x = x_hi * 2 + x_lo), y: 4, z: 8, core: 2. Of those that a mesh axis runs over, the one named last changes fastest.
Arguments:
- grad_out: bfloat16 [32, 1024, 6144], P('dp', 'seq'), may hold values from -6 to 6
- queries: bfloat16 [32, 1024, 3072], P('dp', 'seq'), may hold values from -40 to 40
- keys: bfloat16 [32, 1024, 3072], P('dp', 'seq'), may hold values from -12 to 12
- values: bfloat16 [32, 1024, 3072], P('dp', 'seq'), may hold values from -6 to 6
- out_weight: bfloat16 [6144, 3072], P('dp', 'seq'), may hold values from -0.109375 to 0.109375
Outputs:
- query_grad: bfloat16 [32, 1024, 3072], P('dp', 'seq')
- key_grad: bfloat16 [32, 1024, 3072], P('dp', 'seq')
- value_grad: bfloat16 [32, 1024, 3072], P('dp', 'seq')
- weight_grad: float32 [6144, 3072], P('dp', 'seq')
All inputs are finite; a program needn't handle non-finite values.
Results may differ from a plain program's by a relative error of at most 0.03.
Values may be sent and summed in bfloat16 or wider, within the bound.
A program may use at most 128 MiB of HBM per device.

v0:
```python
import math
import jax
import jax.numpy as jnp
from jax import lax
from jax.sharding import PartitionSpec as P

HEAD_DIM = 128


def shards(grad_out, queries, keys, values, out_weight):
    gathered = lax.all_gather(grad_out, "seq", axis=1, tiled=True)[0]
    length = gathered.shape[0]
    features = out_weight.shape[1]
    heads_here = features // HEAD_DIM
    whole_rows = lax.all_gather(out_weight, "dp", axis=0, tiled=True)
    d_full = jnp.dot(gathered, whole_rows, preferred_element_type=jnp.float32)
    d_attn = d_full.astype(jnp.bfloat16)
    query_all, key_all, value_all = (
        lax.all_to_all(queries, "seq", split_axis=2, concat_axis=1, tiled=True),
        lax.all_to_all(keys, "seq", split_axis=2, concat_axis=1, tiled=True),
        lax.all_to_all(values, "seq", split_axis=2, concat_axis=1, tiled=True),
    )
    head_shape = (length, heads_here, HEAD_DIM)
    query_heads = query_all[0].reshape(head_shape)
    key_heads = key_all[0].reshape(head_shape)
    value_heads = value_all[0].reshape(head_shape)
    grad_heads = d_attn.reshape(head_shape)
    block_rows = math.gcd(length, 512)
    block_count = length // block_rows
    block_shape = (block_count, block_rows, heads_here, HEAD_DIM)
    query_blocks = query_heads.reshape(block_shape)
    grad_blocks = grad_heads.reshape(block_shape)
    inverse_root = 1.0 / math.sqrt(HEAD_DIM)
    token_scale = 1.0 / math.sqrt(lax.axis_size("dp") * length)

    def softmax_rows(query_block):
        scores = (
            jnp.einsum("qhd,khd->hqk", query_block, key_heads, preferred_element_type=jnp.float32)
            * inverse_root
        )
        largest = jnp.max(scores, axis=-1, keepdims=True)
        raised = jnp.exp(scores - largest)
        probabilities = raised / jnp.sum(raised, axis=-1, keepdims=True)
        return (probabilities, probabilities.astype(jnp.bfloat16))

    def attend(probs_low):
        return jnp.einsum(
            "hqk,khd->qhd", probs_low, value_heads, preferred_element_type=jnp.float32
        ).astype(jnp.bfloat16)

    def backward(totals, probabilities, probs_low, attended, query_block, grad_block):
        key_sums, value_sums = totals
        value_sums = value_sums + jnp.einsum(
            "hqk,qhd->khd", probs_low, grad_block, preferred_element_type=jnp.float32
        )
        d_probs = jnp.einsum(
            "qhd,khd->hqk", grad_block, value_heads, preferred_element_type=jnp.float32
        )
        row_delta = jnp.sum(grad_block.astype(jnp.float32) * attended.astype(jnp.float32), axis=-1)
        d_scores = probabilities * (d_probs - jnp.transpose(row_delta)[:, :, None])
        scores_low = d_scores.astype(jnp.bfloat16)
        query_part = (
            jnp.einsum("hqk,khd->qhd", scores_low, key_heads, preferred_element_type=jnp.float32)
            * inverse_root
        ).astype(jnp.bfloat16)
        key_sums = key_sums + jnp.einsum(
            "hqk,qhd->khd", scores_low, query_block, preferred_element_type=jnp.float32
        )
        return ((key_sums, value_sums), query_part)

    zero_sums = (jnp.zeros(head_shape, jnp.float32), jnp.zeros(head_shape, jnp.float32))

    def advance(totals, pieces):
        query_block, grad_block = pieces
        probabilities, probs_low = softmax_rows(query_block)
        attended = attend(probs_low)
        totals, query_part = backward(
            totals, probabilities, probs_low, attended, query_block, grad_block
        )
        return (totals, (query_part, attended))

    (key_sums, value_sums), (query_parts, attended_blocks) = lax.scan(
        advance, zero_sums, (query_blocks, grad_blocks)
    )
    attended_all = attended_blocks.reshape(length, features)
    product = lax.dot_general(
        gathered, attended_all, (((0,), (0,)), ((), ())), preferred_element_type=jnp.float32
    )
    weight_grad = lax.psum_scatter(
        (product * token_scale).astype(jnp.bfloat16), "dp", scatter_dimension=0, tiled=True
    ).astype(jnp.float32)
    query_local = query_parts.reshape(1, length, features)
    key_local = (key_sums * inverse_root).astype(jnp.bfloat16).reshape(1, length, features)
    value_local = value_sums.astype(jnp.bfloat16).reshape(1, length, features)
    query_grad, key_grad, value_grad = (
        lax.all_to_all(query_local, "seq", split_axis=1, concat_axis=2, tiled=True),
        lax.all_to_all(key_local, "seq", split_axis=1, concat_axis=2, tiled=True),
        lax.all_to_all(value_local, "seq", split_axis=1, concat_axis=2, tiled=True),
    )
    return (query_grad, key_grad, value_grad, weight_grad)


def solution(mesh):
    in_specs = (
        P("dp", "seq", None),
        P("dp", "seq", None),
        P("dp", "seq", None),
        P("dp", "seq", None),
        P("dp", "seq"),
    )
    out_specs = (P("dp", "seq", None), P("dp", "seq", None), P("dp", "seq", None), P("dp", "seq"))
    return jax.shard_map(shards, mesh=mesh, in_specs=in_specs, out_specs=out_specs, check_vma=False)
```

profile of v0, /device:TPU:8, one launch (start us, length us, event | category | flops | bytes accessed | tf_op | source)
XLA Modules:
  0.0 578.9 jit_solution(2107303295354958740)
XLA Ops:
  8.6 3.7 copy.111
  12.8 16.9 %reduce = bf16[3072,128]{1,0:T(8,128)(2,1)S(1)} reduce(bf16[3072,1,128]{2,1,0:T(2,128)(2,1)S(1)} %bitcast.154, bf16[]{:T(256)} %broadcast.43), dimensions={1}, to_apply=%bitcast.87.reduce_sub_computation | reduce | bytes 1572866
  29.7 1.1 reshape.34
  30.7 5.8 %all-to-all-start = ((bf16[8,2,24576]{2,1,0:T(2,128)(2,1)}), bf16[8,2,24576]{2,1,0:T(2,128)(2,1)S(1)}, u32[]{:S(2)}, u32[]{:S(2)}) async-start(bf16[8,2,24576]{2,1,0:T(2,128)(2,1)} %reshape.34), calls=%async_computation | async-start | bytes 1572864 | tf_op jit(solution)/shard_map/all_to_all | solution.py:19
  36.6 3.7 copy.113
  40.3 16.9 %reduce.1 = bf16[3072,128]{1,0:T(8,128)(2,1)S(1)} reduce(bf16[3072,1,128]{2,1,0:T(2,128)(2,1)S(1)} %bitcast.164, bf16[]{:T(256)} %broadcast.43), dimensions={1}, to_apply=%bitcast.89.reduce_sub_computation | reduce | bytes 1572866
  57.1 1.1 reshape.36
  58.2 5.9 %all-to-all-start.1 = ((bf16[8,2,24576]{2,1,0:T(2,128)(2,1)}), bf16[8,2,24576]{2,1,0:T(2,128)(2,1)}, u32[]{:S(2)}, u32[]{:S(2)}) async-start(bf16[8,2,24576]{2,1,0:T(2,128)(2,1)} %reshape.36), calls=%async_computation.1 | async-start | bytes 1572864 | tf_op jit(solution)/shard_map/all_to_all | solution.py:20
  64.1 3.7 copy.116
  67.8 16.9 %reduce.2 = bf16[3072,128]{1,0:T(8,128)(2,1)S(1)} reduce(bf16[3072,1,128]{2,1,0:T(2,128)(2,1)S(1)} %bitcast.165, bf16[]{:T(256)} %broadcast.43), dimensions={1}, to_apply=%bitcast.91.reduce_sub_computation | reduce | bytes 1572866
  84.7 1.1 reshape.38
  85.8 5.7 all-to-all-start.2
  91.5 5.5 reshape.35
  97.0 1.5 copy.143
  98.6 1.4 copy.112
  100.0 2.7 reshape_reshape_squeeze.3
  102.7 3.0 copy.118
  105.7 5.5 reshape.37
  111.2 1.5 copy.144
  112.8 1.4 copy.114
  114.2 2.2 reshape_squeeze.6
  116.3 2.3 copy.119
  118.6 5.5 reshape.39
  124.2 1.5 copy.145
  125.7 1.4 copy.117
  127.1 2.2 reshape_squeeze.7
  129.2 229.8 %all-gather.3.cloned.1.call-done = bf16[1,1024,6144]{2,1,0:T(8,128)(2,1)} async-done(((bf16[1,128,6144]{2,1,0:T(8,128)(2,1)}), bf16[1,1024,6144]{2,1,0:T(8,128)(2,1)}) %all-gather.3.cloned.1.call-update) | async-done | bytes 12582928 | tf_op jit(solution)/shard_map/all_gather | solution.py:11
  359.0 11.7 %fusion.45 = bf16[1024,384]{1,0:T(8,128)(2,1)} fusion(bf16[6144,384]{1,0:T(8,128)(2,1)} %all-gather.5.cloned.1.call-done, bf16[1,1024,6144]{2,1,0:T(8,128)(2,1)} %all-gather.3.cloned.1.call-done), kind=kOutput, calls=%fused_computation.42 | convolution fusion | flops 4832231424 | bytes 18087936 | tf_op jit(solution)/shard_map/dot_general | solution.py:16
  370.8 3.2 reshape.30
  374.0 2.2 copy.120
  376.2 35.0 %while.17 = (s32[]{:T(128)}, f32[1024,3,128]{0,2,1:T(8,128)S(1)}, f32[1024,3,128]{0,2,1:T(8,128)S(1)}, bf16[2,512,3,128]{3,1,2,0:T(8,128)(2,1)}, bf16[2,512,3,12...) while((s32[]{:T(128)}, f32[1024,3,128]{0,2,1:T(8,128)S(1)}, ...), condition=%wide.region_4.5_spmd.clone, body=%wide.region_0.4_spmd.clone.sunk | while | flops 2433023488 | bytes 94800312 | solution.py:82
  376.4 5.8 %fusion.91 = (f32[3,512]{1,0:T(4,128)S(1)}, f32[3,512,1024]{2,1,0:T(8,128)}) fusion(bf16[1024,3,128]{2,0,1:T(8,128)(2,1)} %get-tuple-element.279, bf16[2,512,3,128]{3,1,2,0:T(8,128)(2,1)} %get-tuple-element.278, s32[]{:T(128)S(6)} %copy.157), kind=kOutput, calls=%fused_computation.43.clone.1 | convolution fusion | flops 407372800 | bytes 7477252 | tf_op jit(solution)/shard_map/while/body/eval_jaxpr/sub | solution.py:42
  382.2 3.6 fusion.92
  385.9 1.1 multiply_reduce_fusion.3
  389.0 1.2 multiply_convert_fusion.4
  390.4 1.1 fusion.93
  393.9 5.8 %fusion.91 = (f32[3,512]{1,0:T(4,128)S(1)}, f32[3,512,1024]{2,1,0:T(8,128)}) fusion(bf16[1024,3,128]{2,0,1:T(8,128)(2,1)} %get-tuple-element.279, bf16[2,512,3,128]{3,1,2,0:T(8,128)(2,1)} %get-tuple-element.278, s32[]{:T(128)S(6)} %copy.157), kind=kOutput, calls=%fused_computation.43.clone.1 | convolution fusion | flops 407372800 | bytes 7477252 | tf_op jit(solution)/shard_map/while/body/eval_jaxpr/sub | solution.py:42
  399.7 3.6 fusion.92
  403.3 1.1 multiply_reduce_fusion.3
  406.4 1.2 multiply_convert_fusion.4
  407.8 1.1 fusion.93
  411.3 3.0 copy.128
  414.3 1.3 copy.149
  415.6 11.3 %fusion.42 = bf16[6144,384]{0,1:T(8,128)(2,1)} fusion(bf16[1024,384]{0,1:T(8,128)(2,1)S(1)} %bitcast.178, bf16[1,1024,6144]{2,1,0:T(8,128)(2,1)} %all-gather.3.cloned.1.call-done), kind=kOutput, calls=%fused_computation.40 | convolution fusion | flops 4836556800 | bytes 18087936 | tf_op jit(solution)/shard_map/dot_general | solution.py:86
  426.9 6.6 %copy.140 = bf16[6144,384]{1,0:T(8,128)(2,1)} copy(bf16[6144,384]{0,1:T(8,128)(2,1)} %fusion.42) | data formatting | bytes 9437184
  434.6 4.5 copy.124
  439.1 6.2 %reduce.4 = bf16[1024,384]{1,0:T(8,128)(2,1)} reduce(bf16[1024,1,384]{2,1,0:T(2,128)(2,1)S(1)} %bitcast.159, bf16[]{:T(256)} %broadcast.43), dimensions={1}, to_apply=%bitcast.95.reduce_sub_computation | reduce | bytes 1572866
  445.4 2.8 reshape.42
  448.2 5.5 all-to-all-start.4
  453.8 2.2 copy.126
  456.0 5.3 reduce.5
  461.3 1.1 reshape.44
  462.4 2.1 all-to-all-done.4
  464.5 6.2 %all-to-all-start.5 = ((bf16[8,2,24576]{2,1,0:T(2,128)(2,1)}), bf16[8,2,24576]{2,1,0:T(2,128)(2,1)}, u32[]{:S(2)}, u32[]{:S(2)}) async-start(bf16[8,2,24576]{2,1,0:T(2,128)(2,1)} %reshape.44), calls=%async_computation.5 | async-start | bytes 1572864 | tf_op jit(solution)/shard_map/all_to_all | solution.py:98
  472.2 5.3 reduce.3
  477.5 1.1 reshape.40
  478.6 1.8 all-to-all-done.5
  480.4 5.6 all-to-all-start.3
  487.4 1.2 copy.130
  488.5 4.1 reshape.45
  493.2 1.2 copy.131
  494.3 8.4 %all-to-all-done.3 = bf16[8,2,24576]{2,1,0:T(2,128)(2,1)S(1)} async-done(((bf16[8,2,24576]{2,1,0:T(2,128)(2,1)}), bf16[8,2,24576]{2,1,0:T(2,128)(2,1)S(1)}, u32[]{:S(2)}, u32[]{:S(2)}) %all-to-all-start.3) | async-done | bytes 786464 | tf_op jit(solution)/shard_map/all_to_all | solution.py:96
  504.0 1.2 copy.129
  505.2 65.1 %reduce-scatter.4.cloned.1.call-done = bf16[192,384]{1,0:T(8,128)(2,1)} async-done(((bf16[6144,384]{1,0:T(8,128)(2,1)}), bf16[192,384]{1,0:T(8,128)(2,1)}) %reduce-scatter.4.cloned.1.call-update) | async-done | bytes 147472
  (81 shorter events, 18.6 us)
Async XLA Ops:
  7.2 122.1 %all-gather.5.cloned.1.call-start = ((), (), s32[]{:S(2)}) async-start(), calls=%async_computation.8 | async-start | bytes 4866048 | tf_op jit(solution)/shard_map/all_gather | solution.py:15
  7.9 351.1 %all-gather.3.cloned.1.call-start = ((), (), s32[]{:S(2)}) async-start(), calls=%async_computation.7 | async-start | bytes 14155776 | tf_op jit(solution)/shard_map/all_gather | solution.py:11
  30.7 27.5 %all-to-all-start = ((bf16[8,2,24576]{2,1,0:T(2,128)(2,1)}), bf16[8,2,24576]{2,1,0:T(2,128)(2,1)S(1)}, u32[]{:S(2)}, u32[]{:S(2)}) async-start(bf16[8,2,24576]{2,1,0:T(2,128)(2,1)} %reshape.34), calls=%async_computation | async-start | bytes 1572864 | tf_op jit(solution)/shard_map/all_to_all | solution.py:19
  58.2 26.5 %copy-start.2 = (bf16[8,2,24576]{2,1,0:T(2,128)(2,1)}, bf16[8,2,24576]{2,1,0:T(2,128)(2,1)S(1)}, u32[]{:S(2)}) copy-start(bf16[8,2,24576]{2,1,0:T(2,128)(2,1)S(1)} %all-to-all-done) | copy-start | bytes 2359300
  58.2 27.6 %all-to-all-start.1 = ((bf16[8,2,24576]{2,1,0:T(2,128)(2,1)}), bf16[8,2,24576]{2,1,0:T(2,128)(2,1)}, u32[]{:S(2)}, u32[]{:S(2)}) async-start(bf16[8,2,24576]{2,1,0:T(2,128)(2,1)} %reshape.36), calls=%async_computation.1 | async-start | bytes 1572864 | tf_op jit(solution)/shard_map/all_to_all | solution.py:20
  85.8 32.9 %all-to-all-start.2 = ((bf16[8,2,24576]{2,1,0:T(2,128)(2,1)}), bf16[8,2,24576]{2,1,0:T(2,128)(2,1)}, u32[]{:S(2)}, u32[]{:S(2)}) async-start(bf16[8,2,24576]{2,1,0:T(2,128)(2,1)} %reshape.38), calls=%async_computation.2 | async-start | bytes 1572864 | tf_op jit(solution)/shard_map/all_to_all | solution.py:21
  91.5 478.8 %reduce-scatter.4.cloned.1.call-start = ((), (), s32[]{:S(2)}) async-start(), calls=%async_computation.9 | async-start | bytes 4866048
  382.2 3.6 copy-start.1
  382.2 3.6 copy-start.7
  385.9 2.2 slice-start
  387.0 2.0 slice-start.1
  389.0 1.2 copy-start.3
  389.0 1.4 copy-start.6
  390.4 1.1 copy-start
  391.5 1.0 copy-start.4
  391.5 1.4 copy-start.8
  393.0 0.9 copy-start.9
  399.7 3.6 copy-start.1
  399.7 3.6 copy-start.7
  403.3 2.2 slice-start
  404.4 2.0 slice-start.1
  406.4 1.2 copy-start.3
  406.4 1.4 copy-start.6
  407.8 1.1 copy-start
  408.9 1.0 copy-start.4
  408.9 1.4 copy-start.8
  410.4 0.9 copy-start.9
  448.2 16.3 %all-to-all-start.4 = ((bf16[8,2,24576]{2,1,0:T(2,128)(2,1)}), bf16[8,2,24576]{2,1,0:T(2,128)(2,1)S(1)}, u32[]{:S(2)}, u32[]{:S(2)}) async-start(bf16[8,2,24576]{2,1,0:T(2,128)(2,1)} %reshape.42), calls=%async_computation.4 | async-start | bytes 1572864 | tf_op jit(solution)/shard_map/all_to_all | solution.py:97
  461.3 9.4 %copy-start.5 = (bf16[2,512,3,128]{3,1,2,0:T(8,128)(2,1)S(1)}, bf16[2,512,3,128]{3,1,2,0:T(8,128)(2,1)}, u32[]{:S(2)}) copy-start(bf16[2,512,3,128]{3,1,2,0:T(8,128)(2,1)} %get-tuple-element.54) | copy-start | bytes 2359300
  464.5 15.9 %all-to-all-start.5 = ((bf16[8,2,24576]{2,1,0:T(2,128)(2,1)}), bf16[8,2,24576]{2,1,0:T(2,128)(2,1)}, u32[]{:S(2)}, u32[]{:S(2)}) async-start(bf16[8,2,24576]{2,1,0:T(2,128)(2,1)} %reshape.44), calls=%async_computation.5 | async-start | bytes 1572864 | tf_op jit(solution)/shard_map/all_to_all | solution.py:98
  480.4 22.3 %all-to-all-start.3 = ((bf16[8,2,24576]{2,1,0:T(2,128)(2,1)}), bf16[8,2,24576]{2,1,0:T(2,128)(2,1)S(1)}, u32[]{:S(2)}, u32[]{:S(2)}) async-start(bf16[8,2,24576]{2,1,0:T(2,128)(2,1)} %reshape.40), calls=%async_computation.3 | async-start | bytes 1572864 | tf_op jit(solution)/shard_map/all_to_all | solution.py:96
Sparse Core Ops, SparseCore 0:
  10.8 100.1 all-gather.4
  112.8 246.2 all-gather.2
  433.7 136.5 reduce-scatter.3
where the time goes:
time: 589 us; the launch traced here: 579 us
  waiting for transfers between devices  309 us (52%)
  local copies, waits for them, and re-layouts  99.8 us (17%)
  other arithmetic  75.8 us (13%)
  matrix products  45.4 us (8%)
  starting transfers between devices  34.8 us (6%)
  between operations  14.2 us (2%)
    all_gather x1, waiting for transfers between devices, shards(): gathered = lax.all_gather(grad_out, 'seq', axis=1, tiled=True)[0]  230 us
    unnamed x36, local copies, waits for them, and re-layouts  67.8 us
    unnamed x8, other arithmetic  67.5 us
    unnamed x4, waiting for transfers between devices  66.5 us
  transfers between devices with their start and end apart: 9, of which 5 were waited for; matrix products, arithmetic and copies ran while one was open for 25% of the time, Pallas kernels for 0%

commit v1 on v0

--- a/solution.py
+++ b/solution.py
@@ -5,10 +5,13 @@
 from jax.sharding import PartitionSpec as P
 
 HEAD_DIM = 128
+fix_ranges = lambda my_data: jnp.concatenate(
+    lax.all_to_all(jnp.stack([my_data for _ in range(lax.axis_size("seq"))], 0), "seq", 0, 0), 1
+)
 
 
 def shards(grad_out, queries, keys, values, out_weight):
-    gathered = lax.all_gather(grad_out, "seq", axis=1, tiled=True)[0]
+    gathered = fix_ranges(grad_out)[0]
     length = gathered.shape[0]
     features = out_weight.shape[1]
     heads_here = features // HEAD_DIM

time: 589 us -> 497 us (0.84)
  waiting for transfers between devices: 309 us -> 208 us
  local copies, waits for them, and re-layouts: 99.8 us -> 79.2 us
  blocking collectives: 0 us -> 15.5 us
  matrix products: 45.4 us -> 56 us
    all_gather x1 -> x0, waiting for transfers between devices: 230 us -> none  [shards(): gathered = lax.all_gather(grad_out, 'seq', axis=1, tiled=True)[0]]
    all_gather x1, waiting for transfers between devices: 0.01 us -> 94.5 us  [shards(): whole_rows = lax.all_gather(out_weight, 'dp', axis=0, tiled=True)]
    all_to_all x1, waiting for transfers between devices: 0.01 us -> 41.6 us  [lax.all_to_all(jnp.stack([my_data for _ in range(lax.axis_size('seq'))],...]
    unnamed x36 -> x38, local copies, waits for them, and re-layouts: 67.8 us -> 50.9 us
    all_to_all x0 -> x1, blocking collectives: none -> 15.5 us  [shards(): lax.all_to_all(values, 'seq', split_axis=2, concat_axis=1, tiled=True)]
    all_to_all x1, waiting for transfers between devices: 8.36 us -> 0.01 us  [shards(): lax.all_to_all(query_local, 'seq', split_axis=1, concat_axis=2, tiled=True)]
    another operation x0 -> x1, local copies, waits for them, and re-layouts: none -> 7.45 us  [jnp.stack([my_data for _ in range(lax.axis_size('seq'))], 0)]
    dot_general x2, matrix products: 1.92 us -> 8.4 us  [backward(): jnp.einsum('hqk,qhd->khd', scores_low, query_block, preferred_element_typ...]
  transfers between devices with their start and end apart: 9 -> 8, of which waited for: 5 -> 4; matrix products, arithmetic and copies ran while one was open for 25% -> 21% of each run, Pallas kernels for 0% -> 0%
where the time goes in v1:
time: 497 us; the launch traced here: 488 us
  waiting for transfers between devices  208 us (42%)
  local copies, waits for them, and re-layouts  79.2 us (16%)
  other arithmetic  77.6 us (16%)
  matrix products  56 us (11%)
  starting transfers between devices  37 us (7%)
  blocking collectives  15.5 us (3%)
  between operations  14.6 us (3%)
    all_gather x1, waiting for transfers between devices, shards(): whole_rows = lax.all_gather(out_weight, 'dp', axis=0, tiled=True)  94.5 us
    unnamed x8, other arithmetic  69.1 us
    unnamed x3, waiting for transfers between devices  66 us
    unnamed x38, local copies, waits for them, and re-layouts  50.9 us
    all_to_all x1, waiting for transfers between devices, lax.all_to_all(jnp.stack([my_data for _ in range(lax.axis_size('seq'))],...  41.6 us
    all_to_all x1, blocking collectives, shards(): lax.all_to_all(values, 'seq', split_axis=2, concat_axis=1, tiled=True)  15.5 us
    sub x2, matrix products, softmax_rows(): raised = jnp.exp(scores - largest)  11.6 us
    dot_general x1, matrix products, shards(): lax.dot_general(gathered, attended_all, (((0,), (0,)), ((), ())), preferr...  11.3 us
  transfers between devices with their start and end apart: 8, of which 4 were waited for; matrix products, arithmetic and copies ran while one was open for 21% of the time, Pallas kernels for 0%

profile of v1, /device:TPU:8, one launch (start us, length us, event | category | flops | bytes accessed | tf_op | source)
XLA Modules:
  0.0 487.8 jit_solution(5222936832079890006)
XLA Ops:
  7.2 3.7 copy.111
  11.4 16.9 %reduce = bf16[3072,128]{1,0:T(8,128)(2,1)S(1)} reduce(bf16[3072,1,128]{2,1,0:T(2,128)(2,1)S(1)} %bitcast.147, bf16[]{:T(256)} %broadcast.46), dimensions={1}, to_apply=%bitcast.78.reduce_sub_computation | reduce | bytes 1572866
  28.4 1.1 reshape.37
  29.4 5.8 %all-to-all-start = ((bf16[8,2,24576]{2,1,0:T(2,128)(2,1)}), bf16[8,2,24576]{2,1,0:T(2,128)(2,1)S(1)}, u32[]{:S(2)}, u32[]{:S(2)}) async-start(bf16[8,2,24576]{2,1,0:T(2,128)(2,1)} %reshape.37), calls=%async_computation | async-start | bytes 1572864 | tf_op jit(solution)/shard_map/all_to_all | solution.py:22
  35.3 3.7 copy.113
  38.9 16.9 %reduce.1 = bf16[3072,128]{1,0:T(8,128)(2,1)S(1)} reduce(bf16[3072,1,128]{2,1,0:T(2,128)(2,1)S(1)} %bitcast.157, bf16[]{:T(256)} %broadcast.46), dimensions={1}, to_apply=%bitcast.80.reduce_sub_computation | reduce | bytes 1572866
  55.9 1.1 reshape.39
  57.0 5.9 %all-to-all-start.1 = ((bf16[8,2,24576]{2,1,0:T(2,128)(2,1)}), bf16[8,2,24576]{2,1,0:T(2,128)(2,1)}, u32[]{:S(2)}, u32[]{:S(2)}) async-start(bf16[8,2,24576]{2,1,0:T(2,128)(2,1)} %reshape.39), calls=%async_computation.1 | async-start | bytes 1572864 | tf_op jit(solution)/shard_map/all_to_all | solution.py:23
  62.9 3.7 copy.116
  66.6 16.9 %reduce.2 = bf16[3072,128]{1,0:T(8,128)(2,1)S(1)} reduce(bf16[3072,1,128]{2,1,0:T(2,128)(2,1)S(1)} %bitcast.158, bf16[]{:T(256)} %broadcast.46), dimensions={1}, to_apply=%bitcast.82.reduce_sub_computation | reduce | bytes 1572866
  83.7 15.5 %all_to_all.104 = bf16[8,2,24576]{2,1,0:T(2,128)(2,1)S(1)} all-to-all(bf16[8,2,24576]{2,1,0:T(2,128)(2,1)S(1)} %reshape.41), channel_id=1, replica_groups=mesh['dp'=32,'seq'=8] {'seq'}, dimensions={0} | all-to-all | bytes 1572864 | tf_op jit(solution)/shard_map/all_to_all | solution.py:24
  99.2 7.5 %stack.2 = bf16[8,1,128,6144]{3,2,1,0:T(8,128)(2,1)} broadcast(bf16[128,6144]{1,0:T(8,128)(2,1)} %bitcast.171), dimensions={2,3} | broadcast | bytes 14155776 | tf_op jit(solution)/shard_map/stack | solution.py:9
  106.7 7.0 %all-to-all-start.2 = ((bf16[8,1,128,6144]{3,2,1,0:T(8,128)(2,1)}), bf16[8,1,128,6144]{3,2,1,0:T(8,128)(2,1)}, u32[]{:S(2)}, u32[]{:S(2)}) async-start(bf16[8,1,128,6144]{3,2,1,0:T(8,128)(2,1)} %stack.2), calls=%async_computation.2 | async-start | bytes 25165824 | tf_op jit(solution)/shard_map/all_to_all | solution.py:9
  116.3 1.8 copy.118
  118.1 4.1 reshape.40
  123.2 1.2 copy.119
  125.8 1.2 reshape_squeeze.7
  127.0 94.5 %all-gather.2.cloned.1.call-done = bf16[6144,384]{1,0:T(8,128)(2,1)} async-done(((bf16[192,384]{1,0:T(8,128)(2,1)}), bf16[6144,384]{1,0:T(8,128)(2,1)}) %all-gather.2.cloned.1.call-update) | async-done | bytes 4718608 | tf_op jit(solution)/shard_map/all_gather | solution.py:18
  221.6 41.6 %all-to-all-done.2 = bf16[8,1,128,6144]{3,2,1,0:T(8,128)(2,1)} async-done(((bf16[8,1,128,6144]{3,2,1,0:T(8,128)(2,1)}), bf16[8,1,128,6144]{3,2,1,0:T(8,128)(2,1)}, u32[]{:S(2)}, u32[]{:S(2)}) %all-to-all-start.2) | async-done | bytes 12582944 | tf_op jit(solution)/shard_map/all_to_all | solution.py:9
  263.2 11.0 %convolution_convert_fusion.1 = bf16[1024,384]{1,0:T(8,128)(2,1)S(1)} fusion(bf16[1024,6144]{1,0:T(8,128)(2,1)} %bitcast.3, bf16[6144,384]{1,0:T(8,128)(2,1)} %all-gather.2.cloned.1.call-done), kind=kOutput, calls=%fused_computation.38 | convolution fusion | flops 4832231424 | bytes 18087936 | tf_op jit(solution)/shard_map/dot_general | solution.py:19
  274.5 1.0 copy.120
  275.5 46.0 %while.17 = (s32[]{:T(128)}, f32[1024,3,128]{0,2,1:T(8,128)}, f32[1024,3,128]{0,2,1:T(8,128)}, bf16[2,512,3,128]{3,1,2,0:T(8,128)(2,1)}, bf16[2,512,3,128]{3,1,2...) while((s32[]{:T(128)}, f32[1024,3,128]{0,2,1:T(8,128)}, ...), condition=%wide.region_4.5_spmd.clone, body=%wide.region_0.4_spmd.clone.sunk | while | flops 2433023488 | bytes 110530456 | solution.py:85
  275.7 5.8 %fusion.82 = (f32[3,512]{1,0:T(4,128)S(1)}, f32[3,512,1024]{2,1,0:T(8,128)}) fusion(bf16[1024,3,128]{2,0,1:T(8,128)(2,1)} %get-tuple-element.279, bf16[2,512,3,128]{3,1,2,0:T(8,128)(2,1)} %get-tuple-element.278, s32[]{:T(128)} %get-tuple-element.262), kind=kOutput, calls=%fused_computation.39.clone.1 | convolution fusion | flops 407372800 | bytes 7477760 | tf_op jit(solution)/shard_map/while/body/eval_jaxpr/sub | solution.py:45
  281.5 3.7 fusion.83
  285.3 1.1 multiply_reduce_fusion.3
  286.7 2.4 multiply_convert_fusion.4
  289.0 4.0 bitcast_add_fusion.4
  293.0 2.4 fusion.84
  295.4 1.0 bitcast_add_fusion.5
  296.4 1.2 copy-done.3
  298.4 5.8 %fusion.82 = (f32[3,512]{1,0:T(4,128)S(1)}, f32[3,512,1024]{2,1,0:T(8,128)}) fusion(bf16[1024,3,128]{2,0,1:T(8,128)(2,1)} %get-tuple-element.279, bf16[2,512,3,128]{3,1,2,0:T(8,128)(2,1)} %get-tuple-element.278, s32[]{:T(128)} %get-tuple-element.262), kind=kOutput, calls=%fused_computation.39.clone.1 | convolution fusion | flops 407372800 | bytes 7477760 | tf_op jit(solution)/shard_map/while/body/eval_jaxpr/sub | solution.py:45
  304.2 3.7 fusion.83
  307.9 1.1 multiply_reduce_fusion.3
  309.3 2.4 multiply_convert_fusion.4
  311.7 4.4 bitcast_add_fusion.4
  316.1 2.4 fusion.84
  318.5 1.0 bitcast_add_fusion.5
  319.5 1.2 copy-done.3
  321.5 2.3 copy.128
  323.9 11.3 %fusion.36 = bf16[6144,384]{0,1:T(8,128)(2,1)} fusion(bf16[1024,384]{0,1:T(8,128)(2,1)S(1)} %bitcast.172, bf16[1024,6144]{1,0:T(8,128)(2,1)} %bitcast.3), kind=kOutput, calls=%fused_computation.36 | convolution fusion | flops 4836556800 | bytes 18087936 | tf_op jit(solution)/shard_map/dot_general | solution.py:89
  335.2 6.6 %copy.140 = bf16[6144,384]{1,0:T(8,128)(2,1)} copy(bf16[6144,384]{0,1:T(8,128)(2,1)} %fusion.36) | data formatting | bytes 9437184
  341.9 1.1 copy-done.9
  343.7 1.1 reshape.34
  344.8 6.4 %reduce.3 = bf16[1024,384]{1,0:T(8,128)(2,1)} reduce(bf16[1024,1,384]{2,1,0:T(2,128)(2,1)S(1)} %bitcast.152, bf16[]{:T(256)} %broadcast.46), dimensions={1}, to_apply=%bitcast.84.reduce_sub_computation | reduce | bytes 1572866
  351.2 2.8 reshape.43
  354.0 6.5 %all-to-all-start.4 = ((bf16[8,2,24576]{2,1,0:T(2,128)(2,1)}), bf16[8,2,24576]{2,1,0:T(2,128)(2,1)}, u32[]{:S(2)}, u32[]{:S(2)}) async-start(bf16[8,2,24576]{2,1,0:T(2,128)(2,1)} %reshape.43), calls=%async_computation.4 | async-start | bytes 1572864 | tf_op jit(solution)/shard_map/all_to_all | solution.py:99
  360.5 1.0 multiply_convert_fusion.2
  361.5 4.1 copy.124
  365.7 6.4 %reduce.4 = bf16[1024,384]{1,0:T(8,128)(2,1)} reduce(bf16[1024,1,384]{2,1,0:T(2,128)(2,1)S(1)} %bitcast.153, bf16[]{:T(256)} %broadcast.46), dimensions={1}, to_apply=%bitcast.86.reduce_sub_computation | reduce | bytes 1572866
  372.1 2.8 reshape.45
  375.0 5.9 %all-to-all-start.5 = ((bf16[8,2,24576]{2,1,0:T(2,128)(2,1)}), bf16[8,2,24576]{2,1,0:T(2,128)(2,1)S(1)}, u32[]{:S(2)}, u32[]{:S(2)}) async-start(bf16[8,2,24576]{2,1,0:T(2,128)(2,1)} %reshape.45), calls=%async_computation.5 | async-start | bytes 1572864 | tf_op jit(solution)/shard_map/all_to_all | solution.py:100
  381.0 2.2 copy.126
  383.2 5.4 %reduce.5 = bf16[1024,384]{1,0:T(8,128)(2,1)S(1)} reduce(bf16[1024,1,384]{2,1,0:T(2,128)(2,1)S(1)} %bitcast.148, bf16[]{:T(256)} %broadcast.46), dimensions={1}, to_apply=%bitcast.88.reduce_sub_computation | reduce | bytes 1572866
  388.6 1.1 reshape.47
  389.7 5.7 %all-to-all-start.6 = ((bf16[8,2,24576]{2,1,0:T(2,128)(2,1)}), bf16[8,2,24576]{2,1,0:T(2,128)(2,1)S(1)}, u32[]{:S(2)}, u32[]{:S(2)}) async-start(bf16[8,2,24576]{2,1,0:T(2,128)(2,1)} %reshape.47), calls=%async_computation.6 | async-start | bytes 1572864 | tf_op jit(solution)/shard_map/all_to_all | solution.py:101
  395.4 4.1 reshape.44
  399.6 1.0 copy.146
  400.6 1.5 copy.123
  402.1 1.2 copy.129
  404.6 1.2 copy.130
  405.8 5.3 %all-to-all-done.6 = bf16[8,2,24576]{2,1,0:T(2,128)(2,1)S(1)} async-done(((bf16[8,2,24576]{2,1,0:T(2,128)(2,1)}), bf16[8,2,24576]{2,1,0:T(2,128)(2,1)S(1)}, u32[]{:S(2)}, u32[]{:S(2)}) %all-to-all-start.6) | async-done | bytes 786464 | tf_op jit(solution)/shard_map/all_to_all | solution.py:101
  412.4 1.2 copy.131
  413.6 65.3 %reduce-scatter.4.cloned.1.call-done = bf16[192,384]{1,0:T(8,128)(2,1)} async-done(((bf16[6144,384]{1,0:T(8,128)(2,1)}), bf16[192,384]{1,0:T(8,128)(2,1)}) %reduce-scatter.4.cloned.1.call-update) | async-done | bytes 147472
  478.9 1.0 copy.141
  (82 shorter events, 12.4 us)
Async XLA Ops:
  29.4 27.5 %all-to-all-start = ((bf16[8,2,24576]{2,1,0:T(2,128)(2,1)}), bf16[8,2,24576]{2,1,0:T(2,128)(2,1)S(1)}, u32[]{:S(2)}, u32[]{:S(2)}) async-start(bf16[8,2,24576]{2,1,0:T(2,128)(2,1)} %reshape.37), calls=%async_computation | async-start | bytes 1572864 | tf_op jit(solution)/shard_map/all_to_all | solution.py:22
  57.0 26.8 %all-to-all-start.1 = ((bf16[8,2,24576]{2,1,0:T(2,128)(2,1)}), bf16[8,2,24576]{2,1,0:T(2,128)(2,1)}, u32[]{:S(2)}, u32[]{:S(2)}) async-start(bf16[8,2,24576]{2,1,0:T(2,128)(2,1)} %reshape.39), calls=%async_computation.1 | async-start | bytes 1572864 | tf_op jit(solution)/shard_map/all_to_all | solution.py:23
  106.7 156.5 %all-to-all-start.2 = ((bf16[8,1,128,6144]{3,2,1,0:T(8,128)(2,1)}), bf16[8,1,128,6144]{3,2,1,0:T(8,128)(2,1)}, u32[]{:S(2)}, u32[]{:S(2)}) async-start(bf16[8,1,128,6144]{3,2,1,0:T(8,128)(2,1)} %stack.2), calls=%async_computation.2 | async-start | bytes 25165824 | tf_op jit(solution)/shard_map/all_to_all | solution.py:9
  113.7 107.8 %all-gather.2.cloned.1.call-start = ((), (), s32[]{:S(2)}) async-start(), calls=%async_computation.8 | async-start | bytes 4866048 | tf_op jit(solution)/shard_map/all_gather | solution.py:18
  114.4 364.4 %reduce-scatter.4.cloned.1.call-start = ((), (), s32[]{:S(2)}) async-start(), calls=%async_computation.9 | async-start | bytes 4866048
  281.5 4.9 slice-start
  281.5 3.7 copy-start.5
  281.5 3.7 copy-start.10
  281.5 5.1 %slice-start.1 = ((s8[6291456]{0:T(1024)(128)(4,1)}), s8[2097152]{0:T(1024)(128)(4,1)S(1)}, s32[]{:S(2)}) async-start(s8[6291456]{0:T(1024)(128)(4,1)} %bitcast.145), calls=%async_computation.11 | async-start | bytes 4194304 | tf_op jit(solution)/shard_map/while
  289.0 4.0 copy-start
  289.0 4.0 copy-start.7
  293.0 2.4 copy-start.2
  293.0 2.4 copy-start.6
  295.4 1.0 copy-start.8
  296.4 1.2 copy-start.3
  304.2 4.9 slice-start
  304.2 3.7 copy-start.5
  304.2 3.7 copy-start.10
  304.2 5.1 %slice-start.1 = ((s8[6291456]{0:T(1024)(128)(4,1)}), s8[2097152]{0:T(1024)(128)(4,1)S(1)}, s32[]{:S(2)}) async-start(s8[6291456]{0:T(1024)(128)(4,1)} %bitcast.145), calls=%async_computation.11 | async-start | bytes 4194304 | tf_op jit(solution)/shard_map/while
  311.7 4.4 copy-start
  311.7 4.4 copy-start.7
  316.1 2.4 copy-start.2
  316.1 2.4 copy-start.6
  318.5 1.0 copy-start.8
  319.5 1.2 copy-start.3
  341.9 1.1 copy-start.9
  344.7 15.7 %copy-start.1 = (f32[1024,3,128]{0,2,1:T(8,128)S(1)}, f32[1024,3,128]{0,2,1:T(8,128)}, u32[]{:S(2)}) copy-start(f32[1024,3,128]{0,2,1:T(8,128)} %get-tuple-element.55) | copy-start | bytes 4718596
  354.0 20.9 %all-to-all-start.4 = ((bf16[8,2,24576]{2,1,0:T(2,128)(2,1)}), bf16[8,2,24576]{2,1,0:T(2,128)(2,1)}, u32[]{:S(2)}, u32[]{:S(2)}) async-start(bf16[8,2,24576]{2,1,0:T(2,128)(2,1)} %reshape.43), calls=%async_computation.4 | async-start | bytes 1572864 | tf_op jit(solution)/shard_map/all_to_all | solution.py:99
  365.7 15.2 %copy-start.4 = (f32[1024,3,128]{0,2,1:T(8,128)S(1)}, f32[1024,3,128]{0,2,1:T(8,128)}, u32[]{:S(2)}) copy-start(f32[1024,3,128]{0,2,1:T(8,128)} %get-tuple-element.56) | copy-start | bytes 4718596
  375.0 14.8 %all-to-all-start.5 = ((bf16[8,2,24576]{2,1,0:T(2,128)(2,1)}), bf16[8,2,24576]{2,1,0:T(2,128)(2,1)S(1)}, u32[]{:S(2)}, u32[]{:S(2)}) async-start(bf16[8,2,24576]{2,1,0:T(2,128)(2,1)} %reshape.45), calls=%async_computation.5 | async-start | bytes 1572864 | tf_op jit(solution)/shard_map/all_to_all | solution.py:100
  389.7 21.3 %all-to-all-start.6 = ((bf16[8,2,24576]{2,1,0:T(2,128)(2,1)}), bf16[8,2,24576]{2,1,0:T(2,128)(2,1)S(1)}, u32[]{:S(2)}, u32[]{:S(2)}) async-start(bf16[8,2,24576]{2,1,0:T(2,128)(2,1)} %reshape.47), calls=%async_computation.6 | async-start | bytes 1572864 | tf_op jit(solution)/shard_map/all_to_all | solution.py:101
Sparse Core Ops, SparseCore 0:
  117.3 104.2 all-gather.1
  342.0 136.8 reduce-scatter.3
